TPU v7x, 256 devices: a whole 4x4x8 slice. The times are simulated.
256 devices in a mesh: row: 32 (over y, z), col: 8 (over x, core).
Axes of the slice: x: 4, y: 4, z: 8, core: 2. Of those that a mesh axis runs over, the one named last changes fastest.
Arguments:
- tokens: bfloat16 [1536, 8192], P('row', 'col'), may hold values from -6 to 6
- weight: bfloat16 [8192, 32768], P('col', 'row'), may hold values from -0.109375 to 0.109375
- tile_rows: int32 [32, 8, 32], P('row', 'col'), may hold values from 0 to 63, as said below
- tile_cols: int32 [32, 8, 32], P('row', 'col'), may hold values from 0 to 255, as said below
- tile_count: int32 [32, 8], P('row', 'col'), may hold values from 8 to 32, as said below
- hidden_cotangent: bfloat16 [1536, 32768], P('col', 'row'), may hold values from -6 to 6
Outputs:
- hidden: bfloat16 [1536, 32768], P('col', 'row')
- input_grad: bfloat16 [1536, 8192], P('row', 'col')
- weight_grad: bfloat16 [8192, 32768], P('col', 'row')
Inputs may be any that keep to these rules, and one draw needn't show every extreme that they name: tile_rows[r, c, k] is a row block of the weight (tiles of 128 x 128) among the 8 blocks from c * 8 on, which index c of col holds. tile_cols[r, c, k] is a column block among the 8 blocks from r * 8 on, which index r of row holds; the 32 candidate tiles of one device are distinct. The first tile_count[r, c] candidates of device (r, c) are its nonzero tiles; some device holds 32.
All inputs are finite; a program needn't handle non-finite values.
Results may differ from a plain program's by a relative error of at most 0.0049.
Values may be sent and summed in bfloat16 or wider, within the bound.
No kernel may reach another device: no remote copies, remote signals or barrier semaphores. Data moves between devices by JAX's collectives and lax.ppermute only.
A program may use at most 128 MiB of HBM per device.

v0:
```python
import jax
import jax.numpy as jnp
from jax import lax
from jax.sharding import Mesh
from jax.sharding import PartitionSpec as P

TILE = 128
ROW = ("row_0", "row_1")


def laid_out(pieces, dim):
    pieces = jnp.moveaxis(pieces, 0, dim)
    dims = pieces.shape
    return pieces.reshape(*dims[:dim], dims[dim] * dims[dim + 1], *dims[dim + 2 :])


def all_blocks(shard, axes, turns):
    pieces = shard
    for k in turns:
        pieces = lax.all_gather(pieces, axes[k])
    done = turns[::-1]
    back = [done.index(k) for k in range(len(axes))]
    pieces = pieces.transpose(*back, *range(len(axes), pieces.ndim))
    return pieces.reshape(-1, *shard.shape)


def gathered_by_axis(shard, axes, turns, dim):
    return laid_out(all_blocks(shard, axes, turns), dim)


def own_rows(so_far, axes):
    for axis in axes:
        so_far = lax.psum_scatter(so_far, axis, scatter_dimension=0, tiled=True)
    return so_far


def sparse_apply(inputs, live_tiles, in_index, out_index, out_blocks, flipped):
    count_rows, in_width = inputs.shape
    in_blocks = in_width // TILE
    block_rows = 128
    picker = (in_index[:, None] == jnp.arange(in_blocks)[None, :]).astype(jnp.bfloat16)
    placer = (out_index[:, None] == jnp.arange(out_blocks)[None, :]).astype(jnp.float32)

    def per_block(rows_block):
        shaped_rows = rows_block.reshape(block_rows, in_blocks, TILE)
        pieces = jnp.einsum(
            "bjp,kj->bkp", shaped_rows, picker, preferred_element_type=jnp.float32
        ).astype(jnp.bfloat16)
        if flipped:
            product = jnp.einsum(
                "bkq,kpq->bkp", pieces, live_tiles, preferred_element_type=jnp.float32
            )
        else:
            product = jnp.einsum(
                "bkp,kpq->bkq", pieces, live_tiles, preferred_element_type=jnp.float32
            )
        placed = jnp.einsum("bkq,kc->bcq", product, placer, precision=lax.Precision.HIGHEST)
        return placed.reshape(block_rows, out_blocks * TILE)

    stacked = inputs.reshape(count_rows // block_rows, block_rows, in_width)
    return lax.map(per_block, stacked).reshape(count_rows, out_blocks * TILE)


def tile_grads(full_tokens, full_grads, local_rows, local_cols, is_live, row_blocks, col_blocks):
    count_rows = full_tokens.shape[0]
    block_rows = 128
    steps_count = count_rows // block_rows
    left_side = full_tokens.reshape(steps_count, block_rows, row_blocks, TILE)
    right_side = full_grads.reshape(steps_count, block_rows, col_blocks, TILE)

    def accumulate(running, block_pair):
        token_block, grad_block = block_pair
        product = jnp.einsum(
            "bkp,bkq->kpq",
            token_block[:, local_rows],
            grad_block[:, local_cols],
            preferred_element_type=jnp.float32,
        )
        return (running + product, None)

    start_sums = jnp.zeros((local_rows.shape[0], TILE, TILE), jnp.float32)
    tile_sums, leftover = lax.scan(accumulate, start_sums, (left_side, right_side))
    tile_sums = tile_sums * is_live[:, None, None].astype(jnp.float32)
    slot_ids = local_rows * col_blocks + local_cols
    placed = (
        jnp.zeros((row_blocks * col_blocks, TILE, TILE), jnp.float32).at[slot_ids].add(tile_sums)
    )
    placed = placed.reshape(row_blocks, col_blocks, TILE, TILE).transpose(0, 2, 1, 3)
    return placed.reshape(row_blocks * TILE, col_blocks * TILE).astype(jnp.bfloat16)


def on_device(tokens, weight, tile_rows, tile_cols, tile_count, hidden_cotangent):
    row_index = lax.axis_index(ROW)
    col_index = lax.axis_index("col")
    row_blocks = weight.shape[0] // TILE
    col_blocks = weight.shape[1] // TILE
    capacity = tile_rows.shape[2]
    local_rows = tile_rows.reshape(capacity) - col_index * row_blocks
    local_cols = tile_cols.reshape(capacity) - row_index * col_blocks
    is_live = jnp.arange(capacity) < tile_count.reshape(())
    shaped = weight.reshape(row_blocks, TILE, col_blocks, TILE)
    live_tiles = shaped[local_rows, :, local_cols, :] * is_live[:, None, None].astype(jnp.bfloat16)
    full_tokens = gathered_by_axis(tokens, ROW, (0, 1), 0)
    pre_act = lax.psum_scatter(
        sparse_apply(full_tokens, live_tiles, local_rows, local_cols, col_blocks, False),
        "col",
        scatter_dimension=0,
        tiled=True,
    )
    gate_value = jax.nn.sigmoid(pre_act)
    hidden = (pre_act * gate_value).astype(jnp.bfloat16)
    silu_slope = gate_value * (1.0 + pre_act * (1.0 - gate_value))
    grad_pre = (hidden_cotangent.astype(jnp.float32) * silu_slope).astype(jnp.bfloat16)
    full_grads = lax.all_gather(grad_pre, "col", axis=0, tiled=True)
    input_grad = own_rows(
        sparse_apply(full_grads, live_tiles, local_cols, local_rows, row_blocks, True), ROW
    ).astype(jnp.bfloat16)
    weight_grad = tile_grads(
        full_tokens, full_grads, local_rows, local_cols, is_live, row_blocks, col_blocks
    )
    return (hidden, input_grad, weight_grad)


def solution(mesh):
    split = Mesh(mesh.devices.reshape(4, 8, mesh.shape["col"]), ("row_0", "row_1", "col"))
    placed = (
        P(ROW, "col"),
        P("col", ROW),
        P(ROW, "col", None),
        P(ROW, "col", None),
        P(ROW, "col"),
        P("col", ROW),
    )
    return jax.shard_map(
        on_device,
        mesh=split,
        in_specs=placed,
        out_specs=(P("col", ROW), P(ROW, "col"), P("col", ROW)),
        check_vma=False,
    )
```

profile of v0, /device:TPU:1, one launch (start us, length us, event | category | flops | bytes accessed | tf_op | source)
XLA Modules:
  0.0 455.6 jit_solution(8898258210480005376)
XLA Ops:
  7.2 13.0 %all-gather = bf16[192,1024]{1,0:T(8,128)(2,1)} all-gather(bf16[48,1024]{1,0:T(8,128)(2,1)} %param.12), channel_id=2, replica_groups=mesh['row_0'=4,'row_1'=8,'col'=8] {'row_0'}, dimensions={0}, use_global_device_ids=true | all-gather | bytes 491520 | tf_op jit(solution)/shard_map/all_gather | solution.py:20
  24.8 44.5 %all-gather.7.cloned.1.call-done = bf16[32,48,1024]{2,1,0:T(8,128)(2,1)} async-done(((bf16[4,48,1024]{2,1,0:T(8,128)(2,1)}), bf16[32,48,1024]{2,1,0:T(8,128)(2,1)}) %all-gather.7.cloned.1.call-update) | async-done | bytes 3145744 | tf_op jit(solution)/shard_map/all_gather | solution.py:20
  69.2 4.1 copy.27
  73.3 3.5 broadcast.138.clone
  76.8 66.5 %while.33 = (s32[]{:T(128)}, f32[12,128,1024]{2,1,0:T(8,128)}, bf16[12,128,1024]{2,1,0:T(8,128)(2,1)}, bf16[32,128,128]{2,1,0:T(8,128)(2,1)S(1)}, s32[32]{0:T(128)S(1)}, /*index=5*/s32[32]{0:T(128)S(1)}, s32[]{:T(128)}) while((s32[]{:T(128)}, f32[12,128,1024]{2,1,0:T(8,128)}, bf16[12,128,1024]{2,1,0:T(8,128)(2,1)}, ...), condition=%wide.region_1.2_spmd.clone, body=%wide.region_0.1_spmd.clone.sunk | while | flops 193463296 | bytes 11273041 | solution.py:61
  79.0 2.4 fusion.79
  84.5 2.4 fusion.79
  90.1 2.4 fusion.79
  95.6 2.4 fusion.79
  101.2 2.4 fusion.79
  106.7 2.4 fusion.79
  112.3 2.4 fusion.79
  117.8 2.4 fusion.79
  123.3 2.4 fusion.79
  128.9 2.4 fusion.79
  134.4 2.4 fusion.79
  140.0 2.4 fusion.79
  143.4 43.4 %reduce-scatter.4.cloned.1.call-done = f32[192,1024]{1,0:T(8,128)} async-done(((f32[1536,1024]{1,0:T(8,128)}), f32[192,1024]{1,0:T(8,128)}) %reduce-scatter.4.cloned.1.call-update) | async-done | bytes 786448 | tf_op jit(solution)/shard_map/reduce_scatter | solution.py:104
  186.8 2.4 multiply_convert_fusion
  189.2 31.1 %all-gather.5.cloned.1.call-done = bf16[1536,1024]{1,0:T(8,128)(2,1)} async-done(((bf16[192,1024]{1,0:T(8,128)(2,1)}), bf16[1536,1024]{1,0:T(8,128)(2,1)}) %all-gather.5.cloned.1.call-update) | async-done | bytes 3145744 | tf_op jit(solution)/shard_map/all_gather | solution.py:114
  220.3 3.5 broadcast.138
  223.8 68.4 %while.34 = (s32[]{:T(128)}, f32[12,128,1024]{2,1,0:T(8,128)}, bf16[12,128,1024]{2,1,0:T(8,128)(2,1)}, bf16[32,128,128]{2,1,0:T(8,128)(2,1)S(1)}, s32[32]{0:T(128)S(1)}, /*index=5*/s32[32]{0:T(128)S(1)}, s32[]{:T(128)}) while((s32[]{:T(128)}, f32[12,128,1024]{2,1,0:T(8,128)}, bf16[12,128,1024]{2,1,0:T(8,128)(2,1)}, ...), condition=%wide.region_4.5_spmd.clone, body=%wide.region_3.4_spmd.clone.sunk | while | flops 193463296 | bytes 11273041 | solution.py:61
  226.2 2.4 fusion.87
  237.6 2.4 fusion.87
  249.0 2.4 fusion.87
  254.7 2.4 fusion.87
  266.1 2.4 fusion.87
  271.8 2.4 fusion.87
  283.2 2.4 fusion.87
  288.9 2.4 fusion.87
  294.1 2.6 copy.39
  296.7 2.5 copy.40
  299.1 59.5 %reduce-scatter.6.cloned.1.call-done = f32[384,1024]{1,0:T(8,128)} async-done(((f32[1536,1024]{1,0:T(8,128)}), f32[384,1024]{1,0:T(8,128)}) %reduce-scatter.6.cloned.1.call-update) | async-done | bytes 1572880 | tf_op jit(solution)/shard_map/reduce_scatter | solution.py:33
  358.6 72.4 %while.35 = (s32[]{:T(128)}, f32[32,128,128]{2,1,0:T(8,128)}, bf16[12,128,8,128]{3,2,1,0:T(8,128)(2,1)}, s32[32]{0:T(128)S(1)}, bf16[12,128,8,128]{3,2,1,0:T(8,1...) while((s32[]{:T(128)}, f32[32,128,128]{2,1,0:T(8,128)}, bf16[12,128,8,128]{3,2,1,0:T(8,128)(2,1)}, ...), condition=%wide.region_8.9_spmd.clone, body=%wide.region_7.8_spmd.clone.sunk | while | flops 135268544 | bytes 12592227 | solution.py:82
  365.9 3.4 select_add_fusion.2
  372.1 3.5 select_add_fusion.2
  378.3 3.5 select_add_fusion.2
  384.5 3.5 select_add_fusion.2
  390.6 3.5 select_add_fusion.2
  396.8 3.4 select_add_fusion.2
  403.0 3.4 select_add_fusion.2
  409.1 3.4 select_add_fusion.2
  415.3 3.4 select_add_fusion.2
  421.4 3.4 select_add_fusion.2
  427.6 3.4 select_add_fusion.2
  432.8 2.5 broadcast_in_dim.11
  435.3 6.3 %scatter_fusion = f32[64,128,128]{2,1,0:T(8,128)} fusion(f32[64,128,128]{2,1,0:T(8,128)} %broadcast_in_dim.11, s32[32]{0:T(128)S(1)} %get-tuple-element.217, f32[32,128,128]{2,1,0:T(8,128)S(1)} %broadcast_multiply_fusion), kind=kCustom, calls=%fused_computation.3 | custom fusion | flops 524288 | bytes 6291584 | tf_op jit(solution)/shard_map/scatter-add | solution.py:86
  441.6 2.6 convert_element_type.74
  (279 shorter events, 133.0 us)
Async XLA Ops:
  7.2 62.1 %all-gather.7.cloned.1.call-start = ((), (), s32[]{:S(2)}) async-start(), calls=%async_computation.7 | async-start | bytes 3538944 | tf_op jit(solution)/shard_map/all_gather | solution.py:20
  20.2 166.5 %reduce-scatter.4.cloned.1.call-start = ((), (), s32[]{:S(2)}) async-start(), calls=%async_computation.3 | async-start | bytes 7077888 | tf_op jit(solution)/shard_map/reduce_scatter | solution.py:104
  22.5 1.3 copy-start.3
  22.5 1.3 copy-start.4
  143.3 43.5 %copy-start.2 = (bf16[192,1024]{1,0:T(8,128)(2,1)S(1)}, bf16[192,1024]{1,0:T(8,128)(2,1)}, u32[]{:S(2)}) copy-start(bf16[192,1024]{1,0:T(8,128)(2,1)} %param.17) | copy-start | bytes 1179652
  143.3 77.0 %all-gather.5.cloned.1.call-start = ((), (), s32[]{:S(2)}) async-start(), calls=%async_computation.4 | async-start | bytes 3538944 | tf_op jit(solution)/shard_map/all_gather | solution.py:114
  189.2 169.4 %reduce-scatter.6.cloned.1.call-start = ((), (), s32[]{:S(2)}) async-start(), calls=%async_computation.5 | async-start | bytes 7864320 | tf_op jit(solution)/shard_map/reduce_scatter | solution.py:33
  292.2 1.9 copy-start
  292.2 155.3 %reduce-scatter.8.cloned.1.call-start = ((), (), s32[]{:S(2)}) async-start(), calls=%async_computation.6 | async-start | bytes 1769472 | tf_op jit(solution)/shard_map/reduce_scatter | solution.py:33
  294.1 2.6 copy-start.1
Sparse Core Ops, SparseCore 0:
  20.4 48.8 all-gather.6
  143.4 43.3 reduce-scatter.3
  189.3 30.9 all-gather.4
  292.4 66.2 reduce-scatter.5
  361.0 35.9 reduce-scatter.7
where the time goes:
time: 457 us; the launch traced here: 456 us
  waiting for transfers between devices  179 us (39%)
  matrix products  127 us (28%)
  local copies, waits for them, and re-layouts  105 us (23%)
  other arithmetic  14.9 us (3%)
  between operations  14.6 us (3%)
  blocking collectives  13 us (3%)
    reduce_scatter x2, waiting for transfers between devices, own_rows(): so_far = lax.psum_scatter(so_far, axis, scatter_dimension=0, tiled=True)  59.5 us
    dot_general x24, matrix products, per_block(): jnp.einsum('bkq,kc->bcq', product, placer, precision=lax.Precision.HIGHEST)  56.6 us
    all_gather x1, waiting for transfers between devices, all_blocks(): pieces = lax.all_gather(pieces, axes[k])  44.5 us
    reduce_scatter x1, waiting for transfers between devices, on_device(): lax.psum_scatter(sparse_apply(full_tokens, live_tiles, local_rows, local_...  43.4 us
    dot_general x12, matrix products, accumulate(): jnp.einsum('bkp,bkq->kpq', token_block[:, local_rows], grad_block[:, loca...  39.8 us
    all_gather x1, waiting for transfers between devices, on_device(): full_grads = lax.all_gather(grad_pre, 'col', axis=0, tiled=True)  31.1 us
    while x48, local copies, waits for them, and re-layouts  24.3 us
    dynamic_update_slice x24, local copies, waits for them, and re-layouts, sparse_apply(): return lax.map(per_block, stacked).reshape(count_rows, out_blocks * TILE)  20.5 us
  transfers between devices with their start and end apart: 5, of which 4 were waited for; matrix products, arithmetic and copies ran while one was open for 21% of the time, Pallas kernels for 0%

commit v1 on v0

--- a/solution.py
+++ b/solution.py
@@ -111,7 +111,8 @@
     hidden = (pre_act * gate_value).astype(jnp.bfloat16)
     silu_slope = gate_value * (1.0 + pre_act * (1.0 - gate_value))
     grad_pre = (hidden_cotangent.astype(jnp.float32) * silu_slope).astype(jnp.bfloat16)
-    full_grads = lax.all_gather(grad_pre, "col", axis=0, tiled=True)
+    repeated = jnp.stack([grad_pre] * lax.axis_size("col"))
+    full_grads = jnp.concatenate(lax.all_to_all(repeated, "col", 0, 0), axis=0)
     input_grad = own_rows(
         sparse_apply(full_grads, live_tiles, local_cols, local_rows, row_blocks, True), ROW
     ).astype(jnp.bfloat16)

time: 457 us -> 471 us (1.031)
  starting transfers between devices: 0.39 us -> 5.84 us
  local copies, waits for them, and re-layouts: 105 us -> 110 us
    all_to_all x0 -> x1, waiting for transfers between devices: none -> 37.7 us  [on_device(): full_grads = jnp.concatenate(lax.all_to_all(repeated, 'col', 0, 0), axis=0)]
    all_gather x1 -> x0, waiting for transfers between devices: 31.1 us -> none  [on_device(): full_grads = lax.all_gather(grad_pre, 'col', axis=0, tiled=True)]
    all_to_all x0 -> x1, starting transfers between devices: none -> 5.53 us  [on_device(): full_grads = jnp.concatenate(lax.all_to_all(repeated, 'col', 0, 0), axis=0)]
    unnamed x14 -> x10, local copies, waits for them, and re-layouts: 10.8 us -> 13 us
  transfers between devices with their start and end apart: 5 -> 5, of which waited for: 4 -> 4; matrix products, arithmetic and copies ran while one was open for 21% -> 22% of each run, Pallas kernels for 0% -> 0%
where the time goes in v1:
time: 471 us; the launch traced here: 469 us
  waiting for transfers between devices  181 us (38%)
  matrix products  127 us (27%)
  local copies, waits for them, and re-layouts  110 us (23%)
  other arithmetic  16 us (3%)
  between operations  14.5 us (3%)
  blocking collectives  13 us (3%)
  starting transfers between devices  5.84 us (1%)
    reduce_scatter x2, waiting for transfers between devices, own_rows(): so_far = lax.psum_scatter(so_far, axis, scatter_dimension=0, tiled=True)  57.4 us
    dot_general x24, matrix products, per_block(): jnp.einsum('bkq,kc->bcq', product, placer, precision=lax.Precision.HIGHEST)  56.6 us
    reduce_scatter x1, waiting for transfers between devices, on_device(): lax.psum_scatter(sparse_apply(full_tokens, live_tiles, local_rows, local_...  43.5 us
    all_gather x1, waiting for transfers between devices, all_blocks(): pieces = lax.all_gather(pieces, axes[k])  42.4 us
    dot_general x12, matrix products, accumulate(): jnp.einsum('bkp,bkq->kpq', token_block[:, local_rows], grad_block[:, loca...  39.8 us
    all_to_all x1, waiting for transfers between devices, on_device(): full_grads = jnp.concatenate(lax.all_to_all(repeated, 'col', 0, 0), axis=0)  37.7 us
    while x48, local copies, waits for them, and re-layouts  24.3 us
    dynamic_update_slice x24, local copies, waits for them, and re-layouts, sparse_apply(): return lax.map(per_block, stacked).reshape(count_rows, out_blocks * TILE)  20.3 us
  transfers between devices with their start and end apart: 5, of which 4 were waited for; matrix products, arithmetic and copies ran while one was open for 22% of the time, Pallas kernels for 0%

profile of v1, /device:TPU:1, one launch (start us, length us, event | category | flops | bytes accessed | tf_op | source)
XLA Modules:
  0.0 469.3 jit_solution(12096203566393115666)
XLA Ops:
  7.2 13.0 %all-gather = bf16[192,1024]{1,0:T(8,128)(2,1)} all-gather(bf16[48,1024]{1,0:T(8,128)(2,1)} %param.12), channel_id=2, replica_groups=mesh['row_0'=4,'row_1'=8,'col'=8] {'row_0'}, dimensions={0}, use_global_device_ids=true | all-gather | bytes 491520 | tf_op jit(solution)/shard_map/all_gather | solution.py:20
  26.8 42.4 %all-gather.4.cloned.1.call-done = bf16[32,48,1024]{2,1,0:T(8,128)(2,1)} async-done(((bf16[4,48,1024]{2,1,0:T(8,128)(2,1)}), bf16[32,48,1024]{2,1,0:T(8,128)(2,1)}) %all-gather.4.cloned.1.call-update) | async-done | bytes 3145744 | tf_op jit(solution)/shard_map/all_gather | solution.py:20
  69.2 4.1 copy.26
  73.3 3.4 broadcast.140.clone
  76.8 66.4 %while.33 = (s32[]{:T(128)}, f32[12,128,1024]{2,1,0:T(8,128)}, bf16[12,128,1024]{2,1,0:T(8,128)(2,1)}, bf16[32,128,128]{2,1,0:T(8,128)(2,1)S(1)}, s32[32]{0:T(128)S(1)}, /*index=5*/s32[32]{0:T(128)S(1)}, s32[]{:T(128)}) while((s32[]{:T(128)}, f32[12,128,1024]{2,1,0:T(8,128)}, bf16[12,128,1024]{2,1,0:T(8,128)(2,1)}, ...), condition=%wide.region_1.2_spmd.clone, body=%wide.region_0.1_spmd.clone.sunk | while | flops 193463296 | bytes 11273041 | solution.py:61
  79.0 2.4 fusion.79
  84.5 2.4 fusion.79
  90.1 2.4 fusion.79
  95.6 2.4 fusion.79
  101.2 2.4 fusion.79
  106.7 2.4 fusion.79
  112.2 2.4 fusion.79
  117.8 2.4 fusion.79
  123.3 2.4 fusion.79
  128.8 2.4 fusion.79
  134.3 2.4 fusion.79
  139.9 2.4 fusion.79
  143.2 43.5 %reduce-scatter.4.cloned.1.call-done = f32[192,1024]{1,0:T(8,128)} async-done(((f32[1536,1024]{1,0:T(8,128)}), f32[192,1024]{1,0:T(8,128)}) %reduce-scatter.4.cloned.1.call-update) | async-done | bytes 786448 | tf_op jit(solution)/shard_map/reduce_scatter | solution.py:104
  191.0 5.5 %all-to-all-start = ((bf16[8,192,1024]{2,1,0:T(8,128)(2,1)}), bf16[8,192,1024]{2,1,0:T(8,128)(2,1)}, u32[]{:S(2)}, u32[]{:S(2)}) async-start(bf16[8,192,1024]{2,1,0:T(8,128)(2,1)} %stack.2), calls=%async_computation.1 | async-start | bytes 6291456 | tf_op jit(solution)/shard_map/all_to_all | solution.py:115
  196.5 37.7 %all-to-all-done = bf16[8,192,1024]{2,1,0:T(8,128)(2,1)} async-done(((bf16[8,192,1024]{2,1,0:T(8,128)(2,1)}), bf16[8,192,1024]{2,1,0:T(8,128)(2,1)}, u32[]{:S(2)}, u32[]{:S(2)}) %all-to-all-start) | async-done | bytes 3145760 | tf_op jit(solution)/shard_map/all_to_all | solution.py:115
  234.2 3.4 broadcast.140
  237.6 68.3 %while.34 = (s32[]{:T(128)}, f32[12,128,1024]{2,1,0:T(8,128)}, bf16[12,128,1024]{2,1,0:T(8,128)(2,1)}, bf16[32,128,128]{2,1,0:T(8,128)(2,1)S(1)}, s32[32]{0:T(128)S(1)}, /*index=5*/s32[32]{0:T(128)S(1)}, s32[]{:T(128)}) while((s32[]{:T(128)}, f32[12,128,1024]{2,1,0:T(8,128)}, bf16[12,128,1024]{2,1,0:T(8,128)(2,1)}, ...), condition=%wide.region_4.5_spmd.clone, body=%wide.region_3.4_spmd.clone.sunk | while | flops 193463296 | bytes 11273041 | solution.py:61
  240.0 2.4 fusion.87
  245.7 2.4 fusion.87
  251.4 2.4 fusion.87
  257.1 2.4 fusion.87
  262.8 2.4 fusion.87
  274.2 2.4 fusion.87
  279.9 2.4 fusion.87
  285.6 2.4 fusion.87
  306.2 4.4 copy.38
  310.6 4.4 copy.39
  315.0 57.4 %reduce-scatter.6.cloned.1.call-done = f32[384,1024]{1,0:T(8,128)} async-done(((f32[1536,1024]{1,0:T(8,128)}), f32[384,1024]{1,0:T(8,128)}) %reduce-scatter.6.cloned.1.call-update) | async-done | bytes 1572880 | tf_op jit(solution)/shard_map/reduce_scatter | solution.py:33
  372.4 72.4 %while.35 = (s32[]{:T(128)}, f32[32,128,128]{2,1,0:T(8,128)}, bf16[12,128,8,128]{3,2,1,0:T(8,128)(2,1)}, s32[32]{0:T(128)S(1)}, bf16[12,128,8,128]{3,2,1,0:T(8,1...) while((s32[]{:T(128)}, f32[32,128,128]{2,1,0:T(8,128)}, bf16[12,128,8,128]{3,2,1,0:T(8,128)(2,1)}, ...), condition=%wide.region_8.9_spmd.clone, body=%wide.region_7.8_spmd.clone.sunk | while | flops 135268544 | bytes 12592227 | solution.py:82
  379.7 3.4 select_add_fusion.2
  385.9 3.5 select_add_fusion.2
  392.1 3.5 select_add_fusion.2
  398.2 3.5 select_add_fusion.2
  404.4 3.5 select_add_fusion.2
  410.6 3.5 select_add_fusion.2
  416.8 3.4 select_add_fusion.2
  422.9 3.4 select_add_fusion.2
  429.1 3.4 select_add_fusion.2
  435.2 3.4 select_add_fusion.2
  441.4 3.4 select_add_fusion.2
  446.6 2.5 broadcast_in_dim.11
  449.1 6.2 %scatter_fusion = f32[64,128,128]{2,1,0:T(8,128)} fusion(f32[64,128,128]{2,1,0:T(8,128)} %broadcast_in_dim.11, s32[32]{0:T(128)S(1)} %get-tuple-element.211, f32[32,128,128]{2,1,0:T(8,128)S(1)} %broadcast_multiply_fusion), kind=kCustom, calls=%fused_computation.3 | custom fusion | flops 524288 | bytes 6291584 | tf_op jit(solution)/shard_map/scatter-add | solution.py:86
  455.3 2.6 convert_element_type.74
  (275 shorter events, 137.5 us)
Async XLA Ops:
  7.2 62.1 %all-gather.4.cloned.1.call-start = ((), (), s32[]{:S(2)}) async-start(), calls=%async_computation.7 | async-start | bytes 3538944 | tf_op jit(solution)/shard_map/all_gather | solution.py:20
  20.2 166.5 %reduce-scatter.4.cloned.1.call-start = ((), (), s32[]{:S(2)}) async-start(), calls=%async_computation.4 | async-start | bytes 7077888 | tf_op jit(solution)/shard_map/reduce_scatter | solution.py:104
  22.5 1.3 copy-start.1
  22.5 1.3 copy-start.2
  143.2 43.5 %copy-start = (bf16[192,1024]{1,0:T(8,128)(2,1)S(1)}, bf16[192,1024]{1,0:T(8,128)(2,1)}, u32[]{:S(2)}) copy-start(bf16[192,1024]{1,0:T(8,128)(2,1)} %param.17) | copy-start | bytes 1179652
  191.0 43.2 %all-to-all-start = ((bf16[8,192,1024]{2,1,0:T(8,128)(2,1)}), bf16[8,192,1024]{2,1,0:T(8,128)(2,1)}, u32[]{:S(2)}, u32[]{:S(2)}) async-start(bf16[8,192,1024]{2,1,0:T(8,128)(2,1)} %stack.2), calls=%async_computation.1 | async-start | bytes 6291456 | tf_op jit(solution)/shard_map/all_to_all | solution.py:115
  196.5 175.9 %reduce-scatter.6.cloned.1.call-start = ((), (), s32[]{:S(2)}) async-start(), calls=%async_computation.5 | async-start | bytes 7864320 | tf_op jit(solution)/shard_map/reduce_scatter | solution.py:33
  306.0 155.2 %reduce-scatter.8.cloned.1.call-start = ((), (), s32[]{:S(2)}) async-start(), calls=%async_computation.6 | async-start | bytes 1769472 | tf_op jit(solution)/shard_map/reduce_scatter | solution.py:33
Sparse Core Ops, SparseCore 0:
  20.4 48.8 all-gather.3
  143.3 43.3 reduce-scatter.3
  306.1 66.2 reduce-scatter.5
  374.8 36.1 reduce-scatter.7
